TPU v7x, 512 devices: a whole 4x8x8 slice. The times are simulated.
512 devices in a mesh: docs: 128 (over y, z, core), split: 4 (over x).
Axes of the slice: x: 4, y: 8, z: 8, core: 2. Of those that a mesh axis runs over, the one named last changes fastest.
Arguments:
- embeddings: bfloat16 [65536, 1024], P(('docs', 'split')), may hold values from -480 to 480
- cluster_id: int32 [65536], P(('docs', 'split')), may hold values from 0 to 255, as said below
- rank: int32 [65536], P(('docs', 'split')), may hold values from 0 to 65535, each once
Outputs:
- dup_score: float32 [65536], P(('docs', 'split'))
Inputs may be any that keep to these rules, and one draw needn't show every extreme that they name: `cluster_id`: cluster c belongs to owner c // 2. In each aligned block of 128 documents (the documents of one device) at most 2 documents belong to any one owner, and one owner receives exactly 2 from every block.
All inputs are finite; a program needn't handle non-finite values.
Results may differ from a plain program's by a relative error of at most 0.00056.
Values may be sent and summed in bfloat16 or wider, within the bound.
No kernel may reach another device: no remote copies, remote signals or barrier semaphores. Data moves between devices by JAX's collectives and lax.ppermute only.
A program may use at most 64 MiB of HBM per device.

v0:
```python
import jax
import jax.numpy as jnp
from jax import lax
from jax.sharding import PartitionSpec as P

D = 1024
CL_DEV = 2
EPSILON = 1e-06


def per_device(embeddings, cluster_id, rank):
    values = embeddings.astype(jnp.float32)
    unit = (values / jnp.sqrt(jnp.sum(values * values, axis=1, keepdims=True) + EPSILON)).astype(
        jnp.bfloat16
    )
    owners = lax.axis_size("docs")
    local_docs = embeddings.shape[0]
    capacity = 2 * local_docs // owners
    slots_all = owners * capacity
    owner = cluster_id // CL_DEV
    onehot = (owner[:, None] == jnp.arange(owners, dtype=jnp.int32)[None, :]).astype(jnp.int32)
    before = jnp.cumsum(onehot, axis=0) - onehot
    slot_index = jnp.sum(before * onehot, axis=1)
    target = owner * capacity + slot_index
    send_rows = jnp.zeros((slots_all, D), jnp.bfloat16).at[target].set(unit)
    send_cluster = jnp.full((slots_all,), -1, jnp.int32).at[target].set(cluster_id)
    send_rank = jnp.zeros((slots_all,), jnp.int32).at[target].set(rank)
    got_rows, got_cluster, got_rank = (
        lax.all_to_all(
            send_rows.reshape(owners, capacity, D), "docs", split_axis=0, concat_axis=0, tiled=True
        ),
        lax.all_to_all(
            send_cluster.reshape(owners, capacity), "docs", split_axis=0, concat_axis=0, tiled=True
        ),
        lax.all_to_all(
            send_rank.reshape(owners, capacity), "docs", split_axis=0, concat_axis=0, tiled=True
        ),
    )
    queries = got_rows.reshape(slots_all, D)
    query_cluster = got_cluster.reshape(slots_all)
    query_rank = got_rank.reshape(slots_all)

    def pair_scores(rows_other):
        return jnp.einsum("qd,kd->qk", queries, rows_other, preferred_element_type=jnp.float32)

    def row_best(rows_other, cluster_other, rank_other):
        scores = pair_scores(rows_other)
        allowed = (query_cluster[:, None] == cluster_other[None, :]) & (
            rank_other[None, :] < query_rank[:, None]
        )
        return jnp.max(jnp.where(allowed, scores, -1.0), axis=1)

    start_best = jnp.full((slots_all,), -1.0, jnp.float32)
    rows_piece = lax.all_gather(queries, "split", axis=0, tiled=True)
    cluster_piece = lax.all_gather(query_cluster, "split", axis=0, tiled=True)
    rank_piece = lax.all_gather(query_rank, "split", axis=0, tiled=True)
    total = rows_piece.shape[0]
    pieces = total // slots_all
    stacked = (
        rows_piece.reshape(pieces, slots_all, D),
        cluster_piece.reshape(pieces, slots_all),
        rank_piece.reshape(pieces, slots_all),
    )

    def advance(top_score, member):
        return (jnp.maximum(top_score, row_best(member[0], member[1], member[2])), None)

    result, _ = lax.scan(advance, start_best, stacked)
    top_score = result
    returned_scores = lax.all_to_all(
        top_score.reshape(owners, capacity), "docs", split_axis=0, concat_axis=0, tiled=True
    )
    return returned_scores.reshape(slots_all)[target]


def solution(mesh):
    placed = (P(("docs", "split"), None), P(("docs", "split")), P(("docs", "split")))
    return jax.shard_map(
        per_device, mesh=mesh, in_specs=placed, out_specs=P(("docs", "split")), check_vma=False
    )
```

profile of v0, /device:TPU:1, one launch (start us, length us, event | category | flops | bytes accessed | tf_op | source)
XLA Modules:
  0.0 138.9 jit_solution(11490728331037051452)
XLA Ops:
  6.5 0.0 all-gather.4.cloned.1.call-start
  6.5 0.7 and_select_fusion
  7.2 0.1 fusion.11
  7.3 0.2 reduce_window_sum.11
  7.5 0.2 select_reduce_fusion
  7.6 0.7 compare_select_fusion
  8.3 1.1 fusion.5
  9.4 1.8 %scatter_custom_fusion.2 = bf16[256,1024]{1,0:T(8,128)(2,1)S(1)} fusion(s32[128]{0:T(128)S(1)} %compare_select_fusion, bf16[128,1024]{1,0:T(8,128)(2,1)} %param.5, f32[128]{0:T(128)S(1)} %add_sqrt_fusion, bf16[]{:T(256)} %constant.41.clone.1), kind=kCustom, calls=%fused_computation.17 | custom fusion | flops 393216 | bytes 786946 | tf_op jit(solution)/shard_map/scatter | solution.py:25
  11.2 0.2 reshape.52
  11.4 37.6 %all_to_all.38 = bf16[128,2,1024]{2,1,0:T(2,128)(2,1)S(1)} all-to-all(bf16[128,2,1024]{2,1,0:T(2,128)(2,1)S(1)} %reshape.52), channel_id=1, replica_groups=mesh['docs'=128,'split'=4] {'docs'}, dimensions={0} | all-to-all | bytes 1048576 | tf_op jit(solution)/shard_map/all_to_all | solution.py:29
  49.1 1.0 reshape.53
  50.1 0.0 all-gather.4.cloned.1.call-update
  50.1 1.1 scatter_custom_fusion.1
  51.2 0.8 all_to_all.28
  51.9 7.2 %all-to-all-start.1 = ((s32[128,1,2]{2,1,0:T(1,128)}), s32[128,1,2]{2,1,0:T(1,128)S(1)}, u32[]{:S(2)}, u32[]{:S(2)}) async-start(s32[128,1,2]{2,1,0:T(1,128)} %bitcast.2), calls=%async_computation.1 | async-start | bytes 131072 | tf_op jit(solution)/shard_map/all_to_all | solution.py:35
  59.1 1.1 scatter_custom_fusion
  60.2 0.8 all_to_all.25
  61.0 9.8 %all-to-all-done.1 = s32[128,1,2]{2,1,0:T(1,128)S(1)} async-done(((s32[128,1,2]{2,1,0:T(1,128)}), s32[128,1,2]{2,1,0:T(1,128)S(1)}, u32[]{:S(2)}, u32[]{:S(2)}) %all-to-all-start.1) | async-done | bytes 1056 | tf_op jit(solution)/shard_map/all_to_all | solution.py:35
  70.8 0.0 copy-start
  70.8 5.7 %all-to-all-start = ((s32[128,1,2]{2,1,0:T(1,128)}), s32[128,1,2]{2,1,0:T(1,128)S(1)}, u32[]{:S(2)}, u32[]{:S(2)}) async-start(s32[128,1,2]{2,1,0:T(1,128)} %bitcast), calls=%async_computation | async-start | bytes 131072 | tf_op jit(solution)/shard_map/all_to_all | solution.py:32
  76.6 0.6 broadcast.46
  77.1 0.8 reduce.10
  78.0 0.1 reshape.94
  78.1 7.7 %all-gather.1 = s32[4,1,256]{2,1,0:T(1,128)S(1)} all-gather(s32[1,1,256]{2,1,0:T(1,128)S(1)} %reshape.94), channel_id=1, replica_groups=mesh['docs'=128,'split'=4] {'split'}, dimensions={0}, use_global_device_ids=true | all-gather | bytes 5120 | tf_op jit(solution)/shard_map/all_gather | solution.py:56
  85.8 2.4 %all-to-all-done = s32[128,1,2]{2,1,0:T(1,128)S(1)} async-done(((s32[128,1,2]{2,1,0:T(1,128)}), s32[128,1,2]{2,1,0:T(1,128)S(1)}, u32[]{:S(2)}, u32[]{:S(2)}) %all-to-all-start) | async-done | bytes 1056 | tf_op jit(solution)/shard_map/all_to_all | solution.py:32
  88.2 0.0 copy-start.1
  88.2 0.8 reduce.9
  89.1 0.1 reshape.92
  89.2 7.7 %all-gather = s32[4,1,256]{2,1,0:T(1,128)S(1)} all-gather(s32[1,1,256]{2,1,0:T(1,128)S(1)} %reshape.92), channel_id=1, replica_groups=mesh['docs'=128,'split'=4] {'split'}, dimensions={0}, use_global_device_ids=true | all-gather | bytes 5120 | tf_op jit(solution)/shard_map/all_gather | solution.py:55
  96.9 0.1 eq.59
  97.1 0.1 lt.37
  97.2 0.0 all-gather.4.cloned.1.call-done
  97.2 0.0 copy-done
  97.2 0.0 copy-done.1
  97.3 6.5 %while.12 = (s32[]{:T(128)}, f32[256]{0:T(256)S(1)}, s32[128,2]{1,0:T(8,128)}, s32[4,256]{1,0:T(4,128)S(1)}, s32[4,256]{1,0:T(4,128)S(1)}, /*index=5*/s32[128,2]...) while((s32[]{:T(128)}, f32[256]{0:T(256)S(1)}, ...), condition=%wide.wide.region_8.9_spmd.clone, body=%wide.wide.region_6.8_spmd.clone.sunk | while | flops 134545664 | bytes 1061507 | solution.py:68
  97.3 1.6 %fusion.25 = f32[256]{0:T(256)S(1)} fusion(bf16[256,1024]{1,0:T(8,128)(2,1)} %get-tuple-element.222, bf16[4,256,1024]{2,1,0:T(8,128)(2,1)} %get-tuple-element.221, s32[]{:T(128)} %get-tuple-element.203, s32[256]{0:T(256)S(1)} %get-tuple-element.223, s32[256]{0:T(256)S(1)} %get-tuple-element.224, s32[256]{0:T(256)S(1)} %bitcast.43, ...), kind=kOutput, calls=%fused_computation.6.clone.clone.1 | convolution fusion | flops 134545152 | bytes 1054208 | tf_op jit(solution)/shard_map/while/body/eval_jaxpr/qd,kd->qk/dot_general | solution.py:44
  98.9 1.6 %fusion.25 = f32[256]{0:T(256)S(1)} fusion(bf16[256,1024]{1,0:T(8,128)(2,1)} %get-tuple-element.222, bf16[4,256,1024]{2,1,0:T(8,128)(2,1)} %get-tuple-element.221, s32[]{:T(128)} %get-tuple-element.203, s32[256]{0:T(256)S(1)} %get-tuple-element.223, s32[256]{0:T(256)S(1)} %get-tuple-element.224, s32[256]{0:T(256)S(1)} %bitcast.43, ...), kind=kOutput, calls=%fused_computation.6.clone.clone.1 | convolution fusion | flops 134545152 | bytes 1054208 | tf_op jit(solution)/shard_map/while/body/eval_jaxpr/qd,kd->qk/dot_general | solution.py:44
  100.5 1.6 %fusion.25 = f32[256]{0:T(256)S(1)} fusion(bf16[256,1024]{1,0:T(8,128)(2,1)} %get-tuple-element.222, bf16[4,256,1024]{2,1,0:T(8,128)(2,1)} %get-tuple-element.221, s32[]{:T(128)} %get-tuple-element.203, s32[256]{0:T(256)S(1)} %get-tuple-element.223, s32[256]{0:T(256)S(1)} %get-tuple-element.224, s32[256]{0:T(256)S(1)} %bitcast.43, ...), kind=kOutput, calls=%fused_computation.6.clone.clone.1 | convolution fusion | flops 134545152 | bytes 1054208 | tf_op jit(solution)/shard_map/while/body/eval_jaxpr/qd,kd->qk/dot_general | solution.py:44
  102.1 1.6 %fusion.25 = f32[256]{0:T(256)S(1)} fusion(bf16[256,1024]{1,0:T(8,128)(2,1)} %get-tuple-element.222, bf16[4,256,1024]{2,1,0:T(8,128)(2,1)} %get-tuple-element.221, s32[]{:T(128)} %get-tuple-element.203, s32[256]{0:T(256)S(1)} %get-tuple-element.223, s32[256]{0:T(256)S(1)} %get-tuple-element.224, s32[256]{0:T(256)S(1)} %bitcast.43, ...), kind=kOutput, calls=%fused_computation.6.clone.clone.1 | convolution fusion | flops 134545152 | bytes 1054208 | tf_op jit(solution)/shard_map/while/body/eval_jaxpr/qd,kd->qk/dot_general | solution.py:44
  103.7 0.8 all_to_all.32
  104.5 12.7 %all-to-all-start.3 = ((f32[128,1,2]{2,1,0:T(1,128)}), f32[128,1,2]{2,1,0:T(1,128)S(1)}, u32[]{:S(2)}, u32[]{:S(2)}) async-start(f32[128,1,2]{2,1,0:T(1,128)} %bitcast.5), calls=%async_computation.3 | async-start | bytes 131072 | tf_op jit(solution)/shard_map/all_to_all | solution.py:70
  117.2 11.6 %all-to-all-done.3 = f32[128,1,2]{2,1,0:T(1,128)S(1)} async-done(((f32[128,1,2]{2,1,0:T(1,128)}), f32[128,1,2]{2,1,0:T(1,128)S(1)}, u32[]{:S(2)}, u32[]{:S(2)}) %all-to-all-start.3) | async-done | bytes 1056 | tf_op jit(solution)/shard_map/all_to_all | solution.py:70
  128.8 0.5 broadcast.48
  129.3 0.8 reduce.11
  130.1 0.1 reshape.55
  130.3 1.8 %gather_fusion = f32[128]{0:T(128)} fusion(f32[256]{0:T(256)S(1)} %reshape.55, s32[1024]{0:T(1024)S(1)} %pad_clamp_fusion), kind=kCustom, calls=%fused_computation | custom fusion | bytes 1536 | tf_op jit(solution)/shard_map/gather | solution.py:73
  (13 shorter events, 0.1 us)
Async XLA Ops:
  6.5 90.7 %all-gather.4.cloned.1.call-start = ((), (), s32[]{:S(2)}) async-start(), calls=%async_computation.4 | async-start | bytes 2621440 | tf_op jit(solution)/shard_map/all_gather | solution.py:54
  51.9 18.9 %all-to-all-start.1 = ((s32[128,1,2]{2,1,0:T(1,128)}), s32[128,1,2]{2,1,0:T(1,128)S(1)}, u32[]{:S(2)}, u32[]{:S(2)}) async-start(s32[128,1,2]{2,1,0:T(1,128)} %bitcast.2), calls=%async_computation.1 | async-start | bytes 131072 | tf_op jit(solution)/shard_map/all_to_all | solution.py:35
  70.8 26.4 %copy-start = (s32[128,1,2]{2,1,0:T(1,128)}, s32[128,1,2]{2,1,0:T(1,128)S(1)}, u32[]{:S(2)}) copy-start(s32[128,1,2]{2,1,0:T(1,128)S(1)} %all-to-all-done.1) | copy-start | bytes 3076
  70.8 17.4 %all-to-all-start = ((s32[128,1,2]{2,1,0:T(1,128)}), s32[128,1,2]{2,1,0:T(1,128)S(1)}, u32[]{:S(2)}, u32[]{:S(2)}) async-start(s32[128,1,2]{2,1,0:T(1,128)} %bitcast), calls=%async_computation | async-start | bytes 131072 | tf_op jit(solution)/shard_map/all_to_all | solution.py:32
  88.2 9.0 %copy-start.1 = (s32[128,1,2]{2,1,0:T(1,128)}, s32[128,1,2]{2,1,0:T(1,128)S(1)}, u32[]{:S(2)}) copy-start(s32[128,1,2]{2,1,0:T(1,128)S(1)} %all-to-all-done) | copy-start | bytes 3076
  104.5 24.3 %all-to-all-start.3 = ((f32[128,1,2]{2,1,0:T(1,128)}), f32[128,1,2]{2,1,0:T(1,128)S(1)}, u32[]{:S(2)}, u32[]{:S(2)}) async-start(f32[128,1,2]{2,1,0:T(1,128)} %bitcast.5), calls=%async_computation.3 | async-start | bytes 131072 | tf_op jit(solution)/shard_map/all_to_all | solution.py:70
Sparse Core Ops, SparseCore 0:
  50.2 29.5 all-gather.3
where the time goes:
time: 139 us
  blocking collectives  53.1 us (38%)
  starting transfers between devices  25.6 us (18%)
  waiting for transfers between devices  23.8 us (17%)
  between operations  13.6 us (10%)
  local copies, waits for them, and re-layouts  9.27 us (7%)
  other arithmetic  7.19 us (5%)
  matrix products  6.24 us (4%)
    all_to_all x1, blocking collectives, per_device(): lax.all_to_all(send_rows.reshape(owners, capacity, D), 'docs', split_axis...  37.6 us
    all_to_all x1, starting transfers between devices, per_device(): lax.all_to_all(top_score.reshape(owners, capacity), 'docs', split_axis=0,...  12.7 us
    all_to_all x1, waiting for transfers between devices, per_device(): lax.all_to_all(top_score.reshape(owners, capacity), 'docs', split_axis=0,...  11.6 us
    all_to_all x1, waiting for transfers between devices, per_device(): lax.all_to_all(send_rank.reshape(owners, capacity), 'docs', split_axis=0,...  9.83 us
    all_gather x1, blocking collectives, per_device(): cluster_piece = lax.all_gather(query_cluster, 'split', axis=0, tiled=True)  7.72 us
    all_gather x1, blocking collectives, per_device(): rank_piece = lax.all_gather(query_rank, 'split', axis=0, tiled=True)  7.71 us
    all_to_all x1, starting transfers between devices, per_device(): lax.all_to_all(send_rank.reshape(owners, capacity), 'docs', split_axis=0,...  7.17 us
    dot_general x4, matrix products, pair_scores(): jnp.einsum('qd,kd->qk', queries, rows_other, preferred_element_type=jnp.f...  6.24 us
  transfers between devices with their start and end apart: 4, of which 3 were waited for; matrix products, arithmetic and copies ran while one was open for 4% of the time, Pallas kernels for 0%

commit v1 on v0

--- a/solution.py
+++ b/solution.py
@@ -52,7 +52,9 @@
 
     start_best = jnp.full((slots_all,), -1.0, jnp.float32)
     rows_piece = lax.all_gather(queries, "split", axis=0, tiled=True)
-    cluster_piece = lax.all_gather(query_cluster, "split", axis=0, tiled=True)
+    cluster_piece = jnp.concatenate(
+        lax.all_to_all(jnp.stack([query_cluster] * lax.axis_size("split")), "split", 0, 0), axis=0
+    )
     rank_piece = lax.all_gather(query_rank, "split", axis=0, tiled=True)
     total = rows_piece.shape[0]
     pieces = total // slots_all

time: 139 us -> 140 us (level)
  waiting for transfers between devices: 23.8 us -> 31.8 us
  blocking collectives: 53.1 us -> 45.5 us
    all_gather x1 -> x0, blocking collectives: 7.72 us -> none  [per_device(): cluster_piece = lax.all_gather(query_cluster, 'split', axis=0, tiled=True)]
    all_to_all x1, waiting for transfers between devices: 2.39 us -> 9.83 us  [per_device(): lax.all_to_all(send_cluster.reshape(owners, capacity), 'docs', split_axis...]
    all_to_all x1, starting transfers between devices: 12.7 us -> 8.29 us  [per_device(): lax.all_to_all(top_score.reshape(owners, capacity), 'docs', split_axis=0,...]
    all_to_all x0 -> x1, starting transfers between devices: none -> 4.01 us  [per_device(): lax.all_to_all(jnp.stack([query_cluster] * lax.axis_size('split')), 'spli...]
    all_to_all x1, starting transfers between devices: 5.71 us -> 7.17 us  [per_device(): lax.all_to_all(send_cluster.reshape(owners, capacity), 'docs', split_axis...]
    all_to_all x1, starting transfers between devices: 7.17 us -> 5.71 us  [per_device(): lax.all_to_all(send_rank.reshape(owners, capacity), 'docs', split_axis=0,...]
  transfers between devices with their start and end apart: 4 -> 5, of which waited for: 3 -> 3; matrix products, arithmetic and copies ran while one was open for 4% -> 4% of each run, Pallas kernels for 0% -> 0%
where the time goes in v1:
time: 140 us; the launch traced here: 139 us
  blocking collectives  45.5 us (32%)
  waiting for transfers between devices  31.8 us (23%)
  starting transfers between devices  25.2 us (18%)
  between operations  13.6 us (10%)
  local copies, waits for them, and re-layouts  9.8 us (7%)
  other arithmetic  6.98 us (5%)
  matrix products  6.24 us (4%)
    all_to_all x1, blocking collectives, per_device(): lax.all_to_all(send_rows.reshape(owners, capacity, D), 'docs', split_axis...  37.6 us
    all_to_all x1, waiting for transfers between devices, per_device(): lax.all_to_all(top_score.reshape(owners, capacity), 'docs', split_axis=0,...  11.7 us
    all_to_all x1, waiting for transfers between devices, per_device(): lax.all_to_all(send_rank.reshape(owners, capacity), 'docs', split_axis=0,...  10.3 us
    all_to_all x1, waiting for transfers between devices, per_device(): lax.all_to_all(send_cluster.reshape(owners, capacity), 'docs', split_axis...  9.83 us
    all_to_all x1, starting transfers between devices, per_device(): lax.all_to_all(top_score.reshape(owners, capacity), 'docs', split_axis=0,...  8.29 us
    all_gather x1, blocking collectives, per_device(): rank_piece = lax.all_gather(query_rank, 'split', axis=0, tiled=True)  7.91 us
    all_to_all x1, starting transfers between devices, per_device(): lax.all_to_all(send_cluster.reshape(owners, capacity), 'docs', split_axis...  7.17 us
    dot_general x4, matrix products, pair_scores(): jnp.einsum('qd,kd->qk', queries, rows_other, preferred_element_type=jnp.f...  6.24 us
  transfers between devices with their start and end apart: 5, of which 3 were waited for; matrix products, arithmetic and copies ran while one was open for 4% of the time, Pallas kernels for 0%

profile of v1, /device:TPU:1, one launch (start us, length us, event | category | flops | bytes accessed | tf_op | source)
XLA Modules:
  0.0 139.3 jit_solution(9963439865918303955)
XLA Ops:
  6.5 0.0 all-gather.3.cloned.1.call-start
  6.5 0.7 and_select_fusion
  7.2 0.1 fusion.11
  7.3 0.2 reduce_window_sum.11
  7.5 0.2 select_reduce_fusion
  7.6 0.7 compare_select_fusion
  8.3 1.1 fusion.5
  9.4 1.8 %scatter_custom_fusion.2 = bf16[256,1024]{1,0:T(8,128)(2,1)S(1)} fusion(s32[128]{0:T(128)S(1)} %compare_select_fusion, bf16[128,1024]{1,0:T(8,128)(2,1)} %param.5, f32[128]{0:T(128)S(1)} %add_sqrt_fusion, bf16[]{:T(256)} %constant.41.clone.1), kind=kCustom, calls=%fused_computation.17 | custom fusion | flops 393216 | bytes 786946 | tf_op jit(solution)/shard_map/scatter | solution.py:25
  11.2 0.2 reshape.53
  11.4 37.6 %all_to_all.47 = bf16[128,2,1024]{2,1,0:T(2,128)(2,1)S(1)} all-to-all(bf16[128,2,1024]{2,1,0:T(2,128)(2,1)S(1)} %reshape.53), channel_id=1, replica_groups=mesh['docs'=128,'split'=4] {'docs'}, dimensions={0} | all-to-all | bytes 1048576 | tf_op jit(solution)/shard_map/all_to_all | solution.py:29
  49.1 1.0 reshape.54
  50.1 0.0 all-gather.3.cloned.1.call-update
  50.1 1.1 scatter_custom_fusion
  51.2 0.8 all_to_all.31
  51.9 7.2 %all-to-all-start = ((s32[128,1,2]{2,1,0:T(1,128)}), s32[128,1,2]{2,1,0:T(1,128)S(1)}, u32[]{:S(2)}, u32[]{:S(2)}) async-start(s32[128,1,2]{2,1,0:T(1,128)} %bitcast), calls=%async_computation | async-start | bytes 131072 | tf_op jit(solution)/shard_map/all_to_all | solution.py:32
  59.1 1.1 scatter_custom_fusion.1
  60.2 0.8 all_to_all.36
  61.0 9.8 %all-to-all-done = s32[128,1,2]{2,1,0:T(1,128)S(1)} async-done(((s32[128,1,2]{2,1,0:T(1,128)}), s32[128,1,2]{2,1,0:T(1,128)S(1)}, u32[]{:S(2)}, u32[]{:S(2)}) %all-to-all-start) | async-done | bytes 1056 | tf_op jit(solution)/shard_map/all_to_all | solution.py:32
  70.8 0.0 copy-start
  70.8 5.7 %all-to-all-start.2 = ((s32[128,1,2]{2,1,0:T(1,128)}), s32[128,1,2]{2,1,0:T(1,128)S(1)}, u32[]{:S(2)}, u32[]{:S(2)}) async-start(s32[128,1,2]{2,1,0:T(1,128)} %bitcast.2), calls=%async_computation.2 | async-start | bytes 131072 | tf_op jit(solution)/shard_map/all_to_all | solution.py:35
  76.5 0.5 broadcast.50
  77.1 0.7 reduce.9
  77.8 0.1 stack.5
  77.9 10.3 %all-to-all-done.2 = s32[128,1,2]{2,1,0:T(1,128)S(1)} async-done(((s32[128,1,2]{2,1,0:T(1,128)}), s32[128,1,2]{2,1,0:T(1,128)S(1)}, u32[]{:S(2)}, u32[]{:S(2)}) %all-to-all-start.2) | async-done | bytes 1056 | tf_op jit(solution)/shard_map/all_to_all | solution.py:35
  88.2 0.0 copy-start.1
  88.2 0.6 stack.6
  88.8 4.0 %all-to-all-start.1 = ((s32[4,1,256]{2,1,0:T(1,128)}), s32[4,1,256]{2,1,0:T(1,128)S(1)}, u32[]{:S(2)}, u32[]{:S(2)}) async-start(s32[4,1,256]{2,1,0:T(1,128)} %stack.6), calls=%async_computation.1 | async-start | bytes 8192 | tf_op jit(solution)/shard_map/all_to_all | solution.py:56
  92.8 0.7 reduce.10
  93.6 0.1 reshape.93
  93.7 7.9 %all-gather = s32[4,1,256]{2,1,0:T(1,128)S(1)} all-gather(s32[1,1,256]{2,1,0:T(1,128)S(1)} %reshape.93), channel_id=1, replica_groups=mesh['docs'=128,'split'=4] {'split'}, dimensions={0}, use_global_device_ids=true | all-gather | bytes 5120 | tf_op jit(solution)/shard_map/all_gather | solution.py:58
  101.6 0.1 eq.59
  101.8 0.1 lt.37
  101.9 0.0 all-to-all-done.1
  101.9 0.0 all-gather.3.cloned.1.call-done
  102.0 0.0 copy-done
  102.0 0.0 copy-done.1
  102.0 6.5 %while.12 = (s32[]{:T(128)}, f32[256]{0:T(256)S(1)}, s32[128,2]{1,0:T(8,128)}, s32[4,256]{1,0:T(4,128)S(1)}, s32[4,256]{1,0:T(4,128)S(1)}, /*index=5*/s32[128,2]...) while((s32[]{:T(128)}, f32[256]{0:T(256)S(1)}, ...), condition=%wide.wide.region_8.9_spmd.clone, body=%wide.wide.region_6.8_spmd.clone.sunk | while | flops 134545664 | bytes 1061507 | solution.py:70
  102.0 1.6 %fusion.25 = f32[256]{0:T(256)S(1)} fusion(bf16[256,1024]{1,0:T(8,128)(2,1)} %get-tuple-element.222, bf16[4,256,1024]{2,1,0:T(8,128)(2,1)} %get-tuple-element.221, s32[]{:T(128)} %get-tuple-element.203, s32[256]{0:T(256)S(1)} %get-tuple-element.223, s32[256]{0:T(256)S(1)} %get-tuple-element.224, s32[256]{0:T(256)S(1)} %bitcast.43, ...), kind=kOutput, calls=%fused_computation.6.clone.clone.1 | convolution fusion | flops 134545152 | bytes 1054208 | tf_op jit(solution)/shard_map/while/body/eval_jaxpr/qd,kd->qk/dot_general | solution.py:44
  103.6 1.6 %fusion.25 = f32[256]{0:T(256)S(1)} fusion(bf16[256,1024]{1,0:T(8,128)(2,1)} %get-tuple-element.222, bf16[4,256,1024]{2,1,0:T(8,128)(2,1)} %get-tuple-element.221, s32[]{:T(128)} %get-tuple-element.203, s32[256]{0:T(256)S(1)} %get-tuple-element.223, s32[256]{0:T(256)S(1)} %get-tuple-element.224, s32[256]{0:T(256)S(1)} %bitcast.43, ...), kind=kOutput, calls=%fused_computation.6.clone.clone.1 | convolution fusion | flops 134545152 | bytes 1054208 | tf_op jit(solution)/shard_map/while/body/eval_jaxpr/qd,kd->qk/dot_general | solution.py:44
  105.2 1.6 %fusion.25 = f32[256]{0:T(256)S(1)} fusion(bf16[256,1024]{1,0:T(8,128)(2,1)} %get-tuple-element.222, bf16[4,256,1024]{2,1,0:T(8,128)(2,1)} %get-tuple-element.221, s32[]{:T(128)} %get-tuple-element.203, s32[256]{0:T(256)S(1)} %get-tuple-element.223, s32[256]{0:T(256)S(1)} %get-tuple-element.224, s32[256]{0:T(256)S(1)} %bitcast.43, ...), kind=kOutput, calls=%fused_computation.6.clone.clone.1 | convolution fusion | flops 134545152 | bytes 1054208 | tf_op jit(solution)/shard_map/while/body/eval_jaxpr/qd,kd->qk/dot_general | solution.py:44
  106.8 1.6 %fusion.25 = f32[256]{0:T(256)S(1)} fusion(bf16[256,1024]{1,0:T(8,128)(2,1)} %get-tuple-element.222, bf16[4,256,1024]{2,1,0:T(8,128)(2,1)} %get-tuple-element.221, s32[]{:T(128)} %get-tuple-element.203, s32[256]{0:T(256)S(1)} %get-tuple-element.223, s32[256]{0:T(256)S(1)} %get-tuple-element.224, s32[256]{0:T(256)S(1)} %bitcast.43, ...), kind=kOutput, calls=%fused_computation.6.clone.clone.1 | convolution fusion | flops 134545152 | bytes 1054208 | tf_op jit(solution)/shard_map/while/body/eval_jaxpr/qd,kd->qk/dot_general | solution.py:44
  108.4 0.8 all_to_all.40
  109.2 8.3 %all-to-all-start.4 = ((f32[128,1,2]{2,1,0:T(1,128)}), f32[128,1,2]{2,1,0:T(1,128)S(1)}, u32[]{:S(2)}, u32[]{:S(2)}) async-start(f32[128,1,2]{2,1,0:T(1,128)} %bitcast.5), calls=%async_computation.4 | async-start | bytes 131072 | tf_op jit(solution)/shard_map/all_to_all | solution.py:72
  117.5 11.7 %all-to-all-done.4 = f32[128,1,2]{2,1,0:T(1,128)S(1)} async-done(((f32[128,1,2]{2,1,0:T(1,128)}), f32[128,1,2]{2,1,0:T(1,128)S(1)}, u32[]{:S(2)}, u32[]{:S(2)}) %all-to-all-start.4) | async-done | bytes 1056 | tf_op jit(solution)/shard_map/all_to_all | solution.py:72
  129.2 0.5 broadcast.52
  129.7 0.8 reduce.11
  130.5 0.1 reshape.56
  130.7 1.8 %gather_fusion = f32[128]{0:T(128)} fusion(f32[256]{0:T(256)S(1)} %reshape.56, s32[1024]{0:T(1024)S(1)} %pad_clamp_fusion), kind=kCustom, calls=%fused_computation | custom fusion | bytes 1536 | tf_op jit(solution)/shard_map/gather | solution.py:75
  (13 shorter events, 0.1 us)
Async XLA Ops:
  6.5 95.4 %all-gather.3.cloned.1.call-start = ((), (), s32[]{:S(2)}) async-start(), calls=%async_computation.5 | async-start | bytes 2621440 | tf_op jit(solution)/shard_map/all_gather | solution.py:54
  51.9 18.9 %all-to-all-start = ((s32[128,1,2]{2,1,0:T(1,128)}), s32[128,1,2]{2,1,0:T(1,128)S(1)}, u32[]{:S(2)}, u32[]{:S(2)}) async-start(s32[128,1,2]{2,1,0:T(1,128)} %bitcast), calls=%async_computation | async-start | bytes 131072 | tf_op jit(solution)/shard_map/all_to_all | solution.py:32
  70.8 31.1 %copy-start = (s32[128,1,2]{2,1,0:T(1,128)}, s32[128,1,2]{2,1,0:T(1,128)S(1)}, u32[]{:S(2)}) copy-start(s32[128,1,2]{2,1,0:T(1,128)S(1)} %all-to-all-done) | copy-start | bytes 3076
  70.8 17.4 %all-to-all-start.2 = ((s32[128,1,2]{2,1,0:T(1,128)}), s32[128,1,2]{2,1,0:T(1,128)S(1)}, u32[]{:S(2)}, u32[]{:S(2)}) async-start(s32[128,1,2]{2,1,0:T(1,128)} %bitcast.2), calls=%async_computation.2 | async-start | bytes 131072 | tf_op jit(solution)/shard_map/all_to_all | solution.py:35
  88.2 13.8 %copy-start.1 = (s32[128,1,2]{2,1,0:T(1,128)}, s32[128,1,2]{2,1,0:T(1,128)S(1)}, u32[]{:S(2)}) copy-start(s32[128,1,2]{2,1,0:T(1,128)S(1)} %all-to-all-done.2) | copy-start | bytes 3076
  88.8 13.1 %all-to-all-start.1 = ((s32[4,1,256]{2,1,0:T(1,128)}), s32[4,1,256]{2,1,0:T(1,128)S(1)}, u32[]{:S(2)}, u32[]{:S(2)}) async-start(s32[4,1,256]{2,1,0:T(1,128)} %stack.6), calls=%async_computation.1 | async-start | bytes 8192 | tf_op jit(solution)/shard_map/all_to_all | solution.py:56
  109.2 20.0 %all-to-all-start.4 = ((f32[128,1,2]{2,1,0:T(1,128)}), f32[128,1,2]{2,1,0:T(1,128)S(1)}, u32[]{:S(2)}, u32[]{:S(2)}) async-start(f32[128,1,2]{2,1,0:T(1,128)} %bitcast.5), calls=%async_computation.4 | async-start | bytes 131072 | tf_op jit(solution)/shard_map/all_to_all | solution.py:72
Sparse Core Ops, SparseCore 0:
  50.2 29.5 all-gather.2
